TPU v7x, 512 devices: a whole 4x8x8 slice. The times are simulated.
512 devices in a mesh: dp: 8 (over y), tm: 64 (over x, z, core).
Axes of the slice: x: 4, y: 8, z: 8, core: 2. Of those that a mesh axis runs over, the one named last changes fastest.
Arguments:
- signal: bfloat16 [8, 8192, 512], P('dp', 'tm'), may hold values from -16 to 16
- conv_weight: bfloat16 [2, 1024, 512], replicated, may hold values from -0.1875 to 0.1875
- res_weight: bfloat16 [2, 256, 768], replicated, may hold values from -0.375 to 0.375
- grad_out: bfloat16 [8, 8192, 512], P('dp', 'tm'), may hold values from -6 to 6
- skip_cotangent: bfloat16 [8, 8192, 256], P('dp', 'tm'), may hold values from -16 to 16
Outputs:
- input_grad: bfloat16 [8, 8192, 512], P('dp', 'tm')
- conv_grad: bfloat16 [2, 1024, 512], P(None, 'tm')
- res_grad: bfloat16 [2, 256, 768], replicated
All inputs are finite; a program needn't handle non-finite values.
Results may differ from a plain program's by a relative error of at most 0.0063.
Values may be sent and summed in bfloat16 or wider, within the bound.
A program may use at most 64 MiB of HBM per device.

v0:
```python
import jax
import jax.numpy as jnp
from jax import lax
from jax.sharding import Mesh
from jax.sharding import PartitionSpec as P

TM = ("tm_0", "tm_1", "tm_2")


def split_up(array, dim, peers):
    shape = array.shape
    parts = array.reshape(*shape[:dim], peers, shape[dim] // peers, *shape[dim + 1 :])
    return jnp.moveaxis(parts, dim, 0)


def sent_and_summed(array, axis, dim):
    peers = lax.axis_size(axis)
    parts = lax.all_to_all(split_up(array, dim, peers), axis, 0, 0, tiled=True)
    return jnp.sum(parts, axis=0)


def sum_by_axis(array, axes, dim):
    far, near = axes
    own = sent_and_summed(split_up(array, dim, lax.axis_size(far)), near, dim + 1)
    return jnp.sum(lax.all_to_all(own, far, 0, 0, tiled=True), axis=0)


def copy_for_each(array, axis):
    copies = jnp.broadcast_to(array, (lax.axis_size(axis), *array.shape))
    return lax.all_to_all(copies, axis, split_axis=0, concat_axis=0, tiled=True)


def over_copies(array, axis):
    return copy_for_each(array, axis).sum(axis=0)


def passed_along(block, axis, distance):
    devices = range(lax.axis_size(axis))
    route = [(i - distance, i) for i in devices if i - distance in devices]
    return lax.ppermute(block, axis, route)


def filled_up(lines, peers):
    spare = -lines.shape[0] % peers
    if not spare:
        return lines
    return jnp.concatenate([lines, jnp.zeros((spare, *lines.shape[1:]), lines.dtype)])


def joined_along(parts, dim):
    shape = list(parts.shape[1:])
    shape[dim] *= parts.shape[0]
    return jnp.moveaxis(parts, 0, dim).reshape(shape)


def gathered_by_axis(array, axes, dim):
    far, near = axes
    initial = copy_for_each(array, far)
    parts = jnp.swapaxes(copy_for_each(initial, near), 0, 1)
    return joined_along(parts.reshape(-1, *array.shape), dim)


def total_of(array, axes):
    lines = array.reshape(-1, array.shape[-1])
    own = sum_by_axis(filled_up(lines, lax.axis_size(axes[0]) * lax.axis_size(axes[1])), axes, 0)
    whole = gathered_by_axis(own, axes, 0)
    return whole[: len(lines)].reshape(array.shape)


def gate_gradients(dh, z, gated):
    tf = jnp.tanh(z[:, :gated])
    sg = jax.nn.sigmoid(z[:, gated:])
    return jnp.concatenate([dh * sg * (1.0 - tf * tf), dh * tf * sg * (1.0 - sg)], axis=1).astype(
        jnp.bfloat16
    )


def reduce_conv(cat_rows, dz):
    piece = sum_by_axis(
        lax.dot_general(cat_rows, dz, (((0,), (0,)), ((), ())), preferred_element_type=jnp.float32),
        (("tm_0", "tm_1"), "tm_2"),
        0,
    )
    return over_copies(piece, "dp")


def body(signal, conv_weight, res_weight, grad_out, skip_cotangent):
    s_dev, t_dev, width = signal.shape
    gated = res_weight.shape[1]
    near = t_dev // 4
    slabs = lax.axis_size(TM) // 8
    count_rows = s_dev * t_dev
    factor = float(count_rows * lax.axis_size("dp") * lax.axis_size(TM)) ** (-0.5)

    def delayed(x, layer):
        if layer == 0:
            got = passed_along(x[:, t_dev - near :, :], TM, 1)
            return jnp.concatenate([got, x[:, : t_dev - near, :]], axis=1)
        return passed_along(x, TM, slabs)

    def shifted_rows(dpast, layer):
        if layer == 0:
            got = passed_along(dpast[:, :near, :], TM, -1)
            return jnp.concatenate([dpast[:, near:, :], got], axis=1)
        return passed_along(dpast, TM, -slabs)

    x = signal
    cats = []
    zvals = []
    hvals = []
    for layer in range(2):
        past = delayed(x, layer)
        cat_rows = jnp.concatenate([past, x], axis=2).reshape(count_rows, 2 * width)
        z = jnp.dot(cat_rows, conv_weight[layer], preferred_element_type=jnp.float32)
        h = (jnp.tanh(z[:, :gated]) * jax.nn.sigmoid(z[:, gated:])).astype(jnp.bfloat16)
        cats.append(cat_rows)
        zvals.append(z)
        hvals.append(h)
        if layer == 0:
            resid = jnp.dot(h, res_weight[0][:, :width], preferred_element_type=jnp.float32)
            x = (
                (x.reshape(count_rows, width).astype(jnp.float32) + resid)
                .astype(jnp.bfloat16)
                .reshape(s_dev, t_dev, width)
            )
    grad = grad_out.reshape(count_rows, width).astype(jnp.float32)
    skip_rows = skip_cotangent.reshape(count_rows, -1)
    conv_parts = [None, None]
    res_parts = [None, None]
    dz_kept = [None, None]
    for layer in (1, 0):
        outer = jnp.concatenate([grad.astype(jnp.bfloat16), skip_rows], axis=1)
        dh = lax.dot_general(
            outer, res_weight[layer], (((1,), (1,)), ((), ())), preferred_element_type=jnp.float32
        )
        dz = gate_gradients(dh, zvals[layer], gated)
        wcat = lax.dot_general(
            dz, conv_weight[layer], (((1,), (1,)), ((), ())), preferred_element_type=jnp.float32
        )
        dpast = wcat[:, :width].astype(jnp.bfloat16).reshape(s_dev, t_dev, width)
        moved = shifted_rows(dpast, layer).reshape(count_rows, width)
        grad = grad + wcat[:, width:] + moved.astype(jnp.float32)
        res_local = lax.dot_general(
            hvals[layer], outer, (((0,), (0,)), ((), ())), preferred_element_type=jnp.float32
        )
        dz_kept[layer] = dz
        res_parts[layer] = res_local
    for layer in range(2):
        conv_parts[layer] = reduce_conv(cats[layer], dz_kept[layer])
    res_total = total_of(jnp.stack(res_parts), ("dp", ("tm_0", "tm_1", "tm_2")))
    input_grad = grad.astype(jnp.bfloat16).reshape(s_dev, t_dev, width)
    conv_grad = (jnp.stack(conv_parts) * factor).astype(jnp.bfloat16)
    res_grad = (res_total * factor).astype(jnp.bfloat16)
    return (input_grad, conv_grad, res_grad)


def solution(mesh):
    split = Mesh(mesh.devices.reshape(mesh.shape["dp"], 4, 8, 2), ("dp", "tm_0", "tm_1", "tm_2"))
    return jax.shard_map(
        body,
        mesh=split,
        in_specs=(P("dp", TM, None), P(), P(), P("dp", TM, None), P("dp", TM, None)),
        out_specs=(P("dp", TM, None), P(None, TM, None), P()),
        check_vma=False,
    )
```

profile of v0, /device:TPU:1, one launch (start us, length us, event | category | flops | bytes accessed | tf_op | source)
XLA Modules:
  0.0 275.3 jit_solution(2120977228978015561)
XLA Ops:
  1.5 5.4 %collective-permute-start = (bf16[1,32,512]{2,1,0:T(8,128)(2,1)S(1)}, bf16[1,32,512]{2,1,0:T(8,128)(2,1)S(1)}, u32[]{:S(2)}, u32[]{:S(2)}) collective-permute-start(bf16[1,32,512]{2,1,0:T(8,128)(2,1)S(1)} %slice.61), channel_id=1, source_target_pairs={{0,1},{1,2},{2,3},{3,4},{4,5},{5,6},{6,7},{7,8},{8,9},{9,10},{10,1... | collective-permute-start | bytes 98312 | tf_op jit(solution)/shard_map/ppermute | solution.py:40
  12.2 8.4 %collective-permute-start.1 = (bf16[1,128,512]{2,1,0:T(8,128)(2,1)S(1)}, bf16[1,128,512]{2,1,0:T(8,128)(2,1)S(1)}, u32[]{:S(2)}, u32[]{:S(2)}) collective-permute-start(bf16[1,128,512]{2,1,0:T(8,128)(2,1)S(1)} %fusion.2), channel_id=1, source_target_pairs={{0,8},{1,9},{2,10},{3,11},{4,12},{5,13},{6,14},{7,15},{8,16},{9,17... | collective-permute-start | bytes 393224 | tf_op jit(solution)/shard_map/ppermute | solution.py:40
  20.8 1.8 collective-permute-done.1
  30.0 9.5 %all_to_all.53 = f32[2,32,16,512]{3,2,1,0:T(8,128)S(1)} all-to-all(f32[2,32,16,512]{3,2,1,0:T(8,128)S(1)} %copy.26), channel_id=1, replica_groups=mesh['dp'=8,'tm_0'=4,'tm_1'=8,'tm_2'=2] {'tm_2'}, dimensions={0} | all-to-all | bytes 4194304 | tf_op jit(solution)/shard_map/all_to_all | solution.py:18
  43.3 6.1 %all_to_all.54 = f32[2,32,16,512]{3,2,1,0:T(8,128)S(1)} all-to-all(f32[2,32,16,512]{3,2,1,0:T(8,128)S(1)} %copy.24), channel_id=1, replica_groups=mesh['dp'=8,'tm_0'=4,'tm_1'=8,'tm_2'=2] {'tm_2'}, dimensions={0} | all-to-all | bytes 4194304 | tf_op jit(solution)/shard_map/all_to_all | solution.py:18
  49.5 12.7 %all-to-all-start.4 = ((f32[32,16,512]{2,1,0:T(8,128)}), f32[32,16,512]{2,1,0:T(8,128)S(1)}, u32[]{:S(2)}, u32[]{:S(2)}) async-start(f32[32,16,512]{2,1,0:T(8,128)} %reduce_sum.77), calls=%async_computation.4 | async-start | bytes 2097152 | tf_op jit(solution)/shard_map/all_to_all | solution.py:25
  64.8 2.1 copy.37
  66.9 20.5 %all-to-all-done.4 = f32[32,16,512]{2,1,0:T(8,128)S(1)} async-done(((f32[32,16,512]{2,1,0:T(8,128)}), f32[32,16,512]{2,1,0:T(8,128)S(1)}, u32[]{:S(2)}, u32[]{:S(2)}) %all-to-all-start.4) | async-done | bytes 1048608 | tf_op jit(solution)/shard_map/all_to_all | solution.py:25
  87.4 9.8 %all-to-all-start.6 = ((f32[64,8,1,768]{3,1,2,0:T(8,128)}), f32[64,8,1,768]{3,1,2,0:T(8,128)}, u32[]{:S(2)}, u32[]{:S(2)}) async-start(f32[64,8,1,768]{3,1,2,0:T(8,128)} %bitcast.95), calls=%async_computation.6 | async-start | bytes 3145728 | tf_op jit(solution)/shard_map/all_to_all | solution.py:18
  98.5 38.4 %all-to-all-done.6 = f32[64,8,1,768]{3,1,2,0:T(8,128)} async-done(((f32[64,8,1,768]{3,1,2,0:T(8,128)}), f32[64,8,1,768]{3,1,2,0:T(8,128)}, u32[]{:S(2)}, u32[]{:S(2)}) %all-to-all-start.6) | async-done | bytes 1572896 | tf_op jit(solution)/shard_map/all_to_all | solution.py:18
  136.9 5.2 %all-to-all-start.1 = ((f32[32,16,512]{2,1,0:T(8,128)}), f32[32,16,512]{2,1,0:T(8,128)S(1)}, u32[]{:S(2)}, u32[]{:S(2)}) async-start(f32[32,16,512]{2,1,0:T(8,128)} %reduce_sum.74), calls=%async_computation.1 | async-start | bytes 2097152 | tf_op jit(solution)/shard_map/all_to_all | solution.py:25
  144.3 23.1 %all-to-all-done.1 = f32[32,16,512]{2,1,0:T(8,128)S(1)} async-done(((f32[32,16,512]{2,1,0:T(8,128)}), f32[32,16,512]{2,1,0:T(8,128)S(1)}, u32[]{:S(2)}, u32[]{:S(2)}) %all-to-all-start.1) | async-done | bytes 1048608 | tf_op jit(solution)/shard_map/all_to_all | solution.py:25
  167.4 6.8 %all-to-all-start.7 = ((f32[8,1,768]{2,1,0:T(1,128)}), f32[8,1,768]{2,1,0:T(1,128)S(1)}, u32[]{:S(2)}, u32[]{:S(2)}) async-start(f32[8,1,768]{2,1,0:T(1,128)} %reduce_sum.81), calls=%async_computation.7 | async-start | bytes 49152 | tf_op jit(solution)/shard_map/all_to_all | solution.py:25
  174.3 6.6 %all-to-all-done.7 = f32[8,1,768]{2,1,0:T(1,128)S(1)} async-done(((f32[8,1,768]{2,1,0:T(1,128)}), f32[8,1,768]{2,1,0:T(1,128)S(1)}, u32[]{:S(2)}, u32[]{:S(2)}) %all-to-all-start.7) | async-done | bytes 24608 | tf_op jit(solution)/shard_map/all_to_all | solution.py:25
  181.6 3.4 %all-to-all-start.5 = ((f32[8,16,512]{2,1,0:T(8,128)}), f32[8,16,512]{2,1,0:T(8,128)S(1)}, u32[]{:S(2)}, u32[]{:S(2)}) async-start(f32[8,16,512]{2,1,0:T(8,128)} %broadcast_in_dim.13), calls=%async_computation.5 | async-start | bytes 524288 | tf_op jit(solution)/shard_map/all_to_all | solution.py:30
  185.1 9.2 %all-to-all-done.5 = f32[8,16,512]{2,1,0:T(8,128)S(1)} async-done(((f32[8,16,512]{2,1,0:T(8,128)}), f32[8,16,512]{2,1,0:T(8,128)S(1)}, u32[]{:S(2)}, u32[]{:S(2)}) %all-to-all-start.5) | async-done | bytes 262176 | tf_op jit(solution)/shard_map/all_to_all | solution.py:30
  194.9 3.3 %all-to-all-start.8 = ((f32[8,1,768]{2,1,0:T(1,128)}), f32[8,1,768]{2,1,0:T(1,128)S(1)}, u32[]{:S(2)}, u32[]{:S(2)}) async-start(f32[8,1,768]{2,1,0:T(1,128)} %broadcast_in_dim.14), calls=%async_computation.8 | async-start | bytes 49152 | tf_op jit(solution)/shard_map/all_to_all | solution.py:30
  198.3 6.6 %all-to-all-done.8 = f32[8,1,768]{2,1,0:T(1,128)S(1)} async-done(((f32[8,1,768]{2,1,0:T(1,128)}), f32[8,1,768]{2,1,0:T(1,128)S(1)}, u32[]{:S(2)}, u32[]{:S(2)}) %all-to-all-start.8) | async-done | bytes 24608 | tf_op jit(solution)/shard_map/all_to_all | solution.py:30
  205.7 3.4 %all-to-all-start.2 = ((f32[8,16,512]{2,1,0:T(8,128)}), f32[8,16,512]{2,1,0:T(8,128)S(1)}, u32[]{:S(2)}, u32[]{:S(2)}) async-start(f32[8,16,512]{2,1,0:T(8,128)} %broadcast_in_dim.12), calls=%async_computation.2 | async-start | bytes 524288 | tf_op jit(solution)/shard_map/all_to_all | solution.py:30
  209.1 9.2 %all-to-all-done.2 = f32[8,16,512]{2,1,0:T(8,128)S(1)} async-done(((f32[8,16,512]{2,1,0:T(8,128)}), f32[8,16,512]{2,1,0:T(8,128)S(1)}, u32[]{:S(2)}, u32[]{:S(2)}) %all-to-all-start.2) | async-done | bytes 262176 | tf_op jit(solution)/shard_map/all_to_all | solution.py:30
  219.6 14.6 %all-to-all-start.9 = ((f32[64,8,1,768]{3,1,2,0:T(8,128)}), f32[64,8,1,768]{3,1,2,0:T(8,128)S(1)}, u32[]{:S(2)}, u32[]{:S(2)}) async-start(f32[64,8,1,768]{3,1,2,0:T(8,128)} %broadcast_in_dim.15), calls=%async_computation.9 | async-start | bytes 3145728 | tf_op jit(solution)/shard_map/all_to_all | solution.py:30
  235.9 2.4 collective-permute-start.3
  238.3 32.4 %collective-permute-done.3 = bf16[1,32,512]{2,1,0:T(8,128)(2,1)S(1)} collective-permute-done((bf16[1,32,512]{2,1,0:T(8,128)(2,1)S(1)}, bf16[1,32,512]{2,1,0:T(8,128)(2,1)S(1)}, u32[]{:S(2)}, u32[]{:S(2)}) %collective-permute-start.3) | collective-permute-done | bytes 32800 | tf_op jit(solution)/shard_map/ppermute | solution.py:40
  272.1 1.9 all-to-all-done.9
  (83 shorter events, 31.3 us)
Async XLA Ops:
  0.6 11.4 %copy-start.4 = (bf16[1,128,512]{2,1,0:T(8,128)(2,1)S(1)}, bf16[1,128,512]{2,1,0:T(8,128)(2,1)}, u32[]{:S(2)}) copy-start(bf16[1,128,512]{2,1,0:T(8,128)(2,1)} %param.5) | copy-start | bytes 393220
  1.5 8.8 %collective-permute-start = (bf16[1,32,512]{2,1,0:T(8,128)(2,1)S(1)}, bf16[1,32,512]{2,1,0:T(8,128)(2,1)S(1)}, u32[]{:S(2)}, u32[]{:S(2)}) collective-permute-start(bf16[1,32,512]{2,1,0:T(8,128)(2,1)S(1)} %slice.61), channel_id=1, source_target_pairs={{0,1},{1,2},{2,3},{3,4},{4,5},{5,6},{6,7},{7,8},{8,9},{9,10},{10,1... | collective-permute-start | bytes 98312 | tf_op jit(solution)/shard_map/ppermute | solution.py:40
  7.9 14.8 %copy-start.2 = (bf16[2,1024,512]{2,1,0:T(8,128)(2,1)S(1)}, bf16[2,1024,512]{2,1,0:T(8,128)(2,1)}, u32[]{:S(2)}) copy-start(bf16[2,1024,512]{2,1,0:T(8,128)(2,1)} %param.6) | copy-start | bytes 6291460
  11.9 12.8 %copy-start.8 = (f32[128,512]{1,0:T(8,128)}, f32[128,512]{1,0:T(8,128)S(1)}, u32[]{:S(2)}) copy-start(f32[128,512]{1,0:T(8,128)S(1)} %fusion.9) | copy-start | bytes 786436
  11.9 11.4 %copy-start.3 = (bf16[1,128,512]{2,1,0:T(8,128)(2,1)S(1)}, bf16[1,128,512]{2,1,0:T(8,128)(2,1)}, u32[]{:S(2)}) copy-start(bf16[1,128,512]{2,1,0:T(8,128)(2,1)} %param.8) | copy-start | bytes 393220
  11.9 11.4 %copy-start.7 = (bf16[1,128,256]{2,1,0:T(8,128)(2,1)S(1)}, bf16[1,128,256]{2,1,0:T(8,128)(2,1)}, u32[]{:S(2)}) copy-start(bf16[1,128,256]{2,1,0:T(8,128)(2,1)} %param.9) | copy-start | bytes 196612
  12.2 12.5 %copy-start.5 = (bf16[1,128,512]{2,1,0:T(8,128)(2,1)}, bf16[1,128,512]{2,1,0:T(8,128)(2,1)S(1)}, u32[]{:S(2)}) copy-start(bf16[1,128,512]{2,1,0:T(8,128)(2,1)S(1)} %fusion.2) | copy-start | bytes 393220
  12.2 10.4 %collective-permute-start.1 = (bf16[1,128,512]{2,1,0:T(8,128)(2,1)S(1)}, bf16[1,128,512]{2,1,0:T(8,128)(2,1)S(1)}, u32[]{:S(2)}, u32[]{:S(2)}) collective-permute-start(bf16[1,128,512]{2,1,0:T(8,128)(2,1)S(1)} %fusion.2), channel_id=1, source_target_pairs={{0,8},{1,9},{2,10},{3,11},{4,12},{5,13},{6,14},{7,15},{8,16},{9,17... | collective-permute-start | bytes 393224 | tf_op jit(solution)/shard_map/ppermute | solution.py:40
  23.3 4.0 %copy-start.16 = (bf16[1,128,512]{2,1,0:T(8,128)(2,1)S(1)}, bf16[1,128,512]{2,1,0:T(8,128)(2,1)}, u32[]{:S(2)}) copy-start(bf16[1,128,512]{2,1,0:T(8,128)(2,1)} %copy-done.15) | copy-start | bytes 393220
  25.3 15.6 %copy-start = (f32[128,1024]{1,0:T(8,128)}, f32[128,1024]{1,0:T(8,128)S(1)}, u32[]{:S(2)}) copy-start(f32[128,1024]{1,0:T(8,128)S(1)} %fusion.3) | copy-start | bytes 1572868
  26.0 14.8 %collective-permute-start.2 = (bf16[1,128,512]{2,1,0:T(8,128)(2,1)}, bf16[1,128,512]{2,1,0:T(8,128)(2,1)S(1)}, u32[]{:S(2)}, u32[]{:S(2)}) collective-permute-start(bf16[1,128,512]{2,1,0:T(8,128)(2,1)} %fusion.25), channel_id=1, source_target_pairs={{8,0},{9,1},{10,2},{11,3},{12,4},{13,5},{14,6},{15,7},{16,8},{17,9... | collective-permute-start | bytes 393224 | tf_op jit(solution)/shard_map/ppermute | solution.py:40
  40.9 1.9 copy-start.6
  49.5 38.0 %all-to-all-start.4 = ((f32[32,16,512]{2,1,0:T(8,128)}), f32[32,16,512]{2,1,0:T(8,128)S(1)}, u32[]{:S(2)}, u32[]{:S(2)}) async-start(f32[32,16,512]{2,1,0:T(8,128)} %reduce_sum.77), calls=%async_computation.4 | async-start | bytes 2097152 | tf_op jit(solution)/shard_map/all_to_all | solution.py:25
  87.4 49.5 %all-to-all-start.6 = ((f32[64,8,1,768]{3,1,2,0:T(8,128)}), f32[64,8,1,768]{3,1,2,0:T(8,128)}, u32[]{:S(2)}, u32[]{:S(2)}) async-start(f32[64,8,1,768]{3,1,2,0:T(8,128)} %bitcast.95), calls=%async_computation.6 | async-start | bytes 3145728 | tf_op jit(solution)/shard_map/all_to_all | solution.py:18
  136.9 30.4 %all-to-all-start.1 = ((f32[32,16,512]{2,1,0:T(8,128)}), f32[32,16,512]{2,1,0:T(8,128)S(1)}, u32[]{:S(2)}, u32[]{:S(2)}) async-start(f32[32,16,512]{2,1,0:T(8,128)} %reduce_sum.74), calls=%async_computation.1 | async-start | bytes 2097152 | tf_op jit(solution)/shard_map/all_to_all | solution.py:25
  167.4 13.5 %all-to-all-start.7 = ((f32[8,1,768]{2,1,0:T(1,128)}), f32[8,1,768]{2,1,0:T(1,128)S(1)}, u32[]{:S(2)}, u32[]{:S(2)}) async-start(f32[8,1,768]{2,1,0:T(1,128)} %reduce_sum.81), calls=%async_computation.7 | async-start | bytes 49152 | tf_op jit(solution)/shard_map/all_to_all | solution.py:25
  181.6 12.7 %all-to-all-start.5 = ((f32[8,16,512]{2,1,0:T(8,128)}), f32[8,16,512]{2,1,0:T(8,128)S(1)}, u32[]{:S(2)}, u32[]{:S(2)}) async-start(f32[8,16,512]{2,1,0:T(8,128)} %broadcast_in_dim.13), calls=%async_computation.5 | async-start | bytes 524288 | tf_op jit(solution)/shard_map/all_to_all | solution.py:30
  194.9 10.1 %all-to-all-start.8 = ((f32[8,1,768]{2,1,0:T(1,128)}), f32[8,1,768]{2,1,0:T(1,128)S(1)}, u32[]{:S(2)}, u32[]{:S(2)}) async-start(f32[8,1,768]{2,1,0:T(1,128)} %broadcast_in_dim.14), calls=%async_computation.8 | async-start | bytes 49152 | tf_op jit(solution)/shard_map/all_to_all | solution.py:30
  205.7 12.7 %all-to-all-start.2 = ((f32[8,16,512]{2,1,0:T(8,128)}), f32[8,16,512]{2,1,0:T(8,128)S(1)}, u32[]{:S(2)}, u32[]{:S(2)}) async-start(f32[8,16,512]{2,1,0:T(8,128)} %broadcast_in_dim.12), calls=%async_computation.2 | async-start | bytes 524288 | tf_op jit(solution)/shard_map/all_to_all | solution.py:30
  218.3 15.9 %copy-start.10 = (bf16[128,256]{1,0:T(8,128)(2,1)S(1)}, bf16[128,256]{1,0:T(8,128)(2,1)}, u32[]{:S(2)}) copy-start(bf16[128,256]{1,0:T(8,128)(2,1)} %copy-done.9) | copy-start | bytes 196612
  218.3 15.9 %copy-start.12 = (bf16[128,256]{1,0:T(8,128)(2,1)S(1)}, bf16[128,256]{1,0:T(8,128)(2,1)}, u32[]{:S(2)}) copy-start(bf16[128,256]{1,0:T(8,128)(2,1)} %copy-done.11) | copy-start | bytes 196612
  219.6 51.1 %copy-start.1 = (f32[128,1024]{1,0:T(8,128)S(1)}, f32[128,1024]{1,0:T(8,128)}, u32[]{:S(2)}) copy-start(f32[128,1024]{1,0:T(8,128)} %copy-done) | copy-start | bytes 1572868
  219.6 54.3 %all-to-all-start.9 = ((f32[64,8,1,768]{3,1,2,0:T(8,128)}), f32[64,8,1,768]{3,1,2,0:T(8,128)S(1)}, u32[]{:S(2)}, u32[]{:S(2)}) async-start(f32[64,8,1,768]{3,1,2,0:T(8,128)} %broadcast_in_dim.15), calls=%async_computation.9 | async-start | bytes 3145728 | tf_op jit(solution)/shard_map/all_to_all | solution.py:30
  235.9 34.7 %collective-permute-start.3 = (bf16[1,32,512]{2,1,0:T(8,128)(2,1)S(1)}, bf16[1,32,512]{2,1,0:T(8,128)(2,1)S(1)}, u32[]{:S(2)}, u32[]{:S(2)}) collective-permute-start(bf16[1,32,512]{2,1,0:T(8,128)(2,1)S(1)} %slice.87), channel_id=1, source_target_pairs={{1,0},{2,1},{3,2},{4,3},{5,4},{6,5},{7,6},{8,7},{9,8},{10,9},{11,1... | collective-permute-start | bytes 98312 | tf_op jit(solution)/shard_map/ppermute | solution.py:40
  (6 other events, 4.9 us)
where the time goes:
time: 277 us; the launch traced here: 275 us
  waiting for transfers between devices  151 us (55%)
  starting transfers between devices  76.7 us (28%)
  blocking collectives  15.7 us (6%)
  local copies, waits for them, and re-layouts  11.4 us (4%)
  matrix products  11.2 us (4%)
  other arithmetic  8.18 us (3%)
    all_to_all x3, waiting for transfers between devices, sum_by_axis(): return jnp.sum(lax.all_to_all(own, far, 0, 0, tiled=True), axis=0)  50.2 us
    all_to_all x1, waiting for transfers between devices, sent_and_summed(): parts = lax.all_to_all(split_up(array, dim, peers), axis, 0, 0, tiled=True)  38.4 us
    ppermute x4, waiting for transfers between devices, passed_along(): return lax.ppermute(block, axis, route)  35.5 us
    all_to_all x4, waiting for transfers between devices, copy_for_each(): return lax.all_to_all(copies, axis, split_axis=0, concat_axis=0, tiled=True)  26.9 us
    all_to_all x3, starting transfers between devices, sum_by_axis(): return jnp.sum(lax.all_to_all(own, far, 0, 0, tiled=True), axis=0)  24.8 us
    all_to_all x4, starting transfers between devices, copy_for_each(): return lax.all_to_all(copies, axis, split_axis=0, concat_axis=0, tiled=True)  24.7 us
    ppermute x4, starting transfers between devices, passed_along(): return lax.ppermute(block, axis, route)  17.4 us
    all_to_all x2, blocking collectives, sent_and_summed(): parts = lax.all_to_all(split_up(array, dim, peers), axis, 0, 0, tiled=True)  15.7 us
  transfers between devices with their start and end apart: 12, of which 11 were waited for; matrix products, arithmetic and copies ran while one was open for 6% of the time, Pallas kernels for 0%

commit v1 on v0

v1 whole, which is shorter than its diff:
```python
import functools

import jax
import jax.numpy as jnp
from jax import lax
from jax.experimental import pallas as pl
from jax.experimental.pallas import tpu as pltpu
from jax.sharding import Mesh
from jax.sharding import PartitionSpec as P

TM = ("tm_0", "tm_1", "tm_2")
NX, NZ, NC = 4, 8, 2
MESH = pl.DeviceIdType.MESH
BF = jnp.bfloat16
F32 = jnp.float32


def mm(a, b):
    return jnp.dot(a, b, preferred_element_type=F32)


def mm_t(a, b):
    return lax.dot_general(a, b, (((1,), (1,)), ((), ())), preferred_element_type=F32)


def t_mm(a, b):
    return lax.dot_general(a, b, (((0,), (0,)), ((), ())), preferred_element_type=F32)


class Links:
    def __init__(self, send, recv, local):
        self.send, self.recv, self.local = send, recv, local
        self.n_remote = self.n_local = 0
        self.sent = []
        self.stored = []

    def push(self, src, dst, device):
        i = self.n_remote
        self.n_remote += 1
        copy = pltpu.make_async_remote_copy(
            src_ref=src,
            dst_ref=dst,
            send_sem=self.send.at[i],
            recv_sem=self.recv.at[i],
            device_id=device,
            device_id_type=MESH,
        )
        copy.start()
        self.sent.append(copy)
        return copy

    def move(self, src, dst, last=False):
        i = self.n_local
        self.n_local += 1
        copy = pltpu.make_async_copy(src, dst, self.local.at[i])
        copy.start()
        if last:
            self.stored.append(copy)
        return copy

    def finish(self):
        for copy in self.sent:
            copy.wait_send()
        for copy in self.stored:
            copy.wait()


def kernel(
    ny, factor,
    sig, cw, rw, go_in, sk_in,
    ig_out, cg_out, rg_out,
    x0, p0, w, r, go, sk, xh, ph, tf0, sg0, hk, hs, dz1, dz1s, dz0, dz0s,
    gp, gpb, dp, dpr, dp0, dp0r, igv,
    cs1, cx1, cz1, czr1, cy1, cyr1,
    cs0, cx0, cz0, czr0, cy0, cyr0, cgv,
    rs, rxr, rz, rzr, ry, ryr, rg, rx, rc,
    send, recv, local,
):
    y = lax.axis_index("dp")
    x = lax.axis_index("tm_0")
    z = lax.axis_index("tm_1")
    c = lax.axis_index("tm_2")
    t = x * (NZ * NC) + z * NC + c
    nt = NX * NZ * NC
    near = 32
    far = 8
    rows, width = 128, 512
    gated = 256

    def at(dy=0, dx=0, dz=0, dc=0):
        return (
            lax.rem(y + dy, ny), lax.rem(x + dx, NX), lax.rem(z + dz, NZ), lax.rem(c + dc, NC)
        )

    def along(d):
        s = lax.rem(t + (d + nt), nt)
        return (y, s // (NZ * NC), lax.rem(s // NC, NZ), lax.rem(s, NC))

    partner = at(dc=1)
    xs = [at(dx=d) for d in range(1, NX)]
    zs = [at(dz=d) for d in range(1, NZ)]
    ys = [at(dy=d) for d in range(1, ny)]
    yc = [(dy, dc) for dy in range(ny) for dc in range(NC) if dy or dc]

    barrier = pltpu.get_barrier_semaphore()
    greeted = [along(1), along(-1), along(far), along(-far)]
    greeted += xs + zs + [at(dy=dy, dc=dc) for dy, dc in yc]
    for device in greeted:
        pl.semaphore_signal(barrier, inc=1, device_id=device, device_id_type=MESH)

    link = Links(send, recv, local)
    own, other = pl.ds(0, rows), pl.ds(rows, rows)
    in_x = link.move(sig.at[0], x0.at[own])
    in_p = link.move(sig.at[0, pl.ds(0, rows - near)], p0.at[pl.ds(near, rows - near)])
    in_w0 = link.move(cw.at[0], w.at[0])
    in_r0 = link.move(rw.at[0], r.at[0])
    in_go = link.move(go_in.at[0], go.at[own])
    in_sk = link.move(sk_in.at[0], sk.at[own])
    in_r1 = link.move(rw.at[1], r.at[1])
    in_w1 = link.move(cw.at[1], w.at[1])

    def layer0(lo, n):
        part = pl.ds(lo, n)
        zv = mm(p0[part, :], w[0, 0:width, :]) + mm(x0[part, :], w[0, width : 2 * width, :])
        tf = jnp.tanh(zv[:, :gated])
        sg = jax.nn.sigmoid(zv[:, gated:])
        h = (tf * sg).astype(BF)
        tf0[part, :] = tf
        sg0[part, :] = sg
        xh[part, width : width + gated] = h
        xh[part, 0:width] = (x0[part, :].astype(F32) + mm(h, r[0, :, 0:width])).astype(BF)

    in_x.wait()
    in_p.wait()
    in_w0.wait()
    in_r0.wait()
    layer0(near, rows - near)
    in_go.wait()
    in_sk.wait()

    pl.semaphore_wait(barrier, len(greeted))
    halo = link.push(x0.at[pl.ds(rows - near, near)], p0.at[pl.ds(0, near)], along(1))
    high = pl.ds(near, rows - near)
    low = pl.ds(0, near)
    far_high = link.push(xh.at[high], ph.at[high], along(far))
    x0_there = link.push(x0.at[own], x0.at[other], partner)
    go_there = link.push(go.at[own], go.at[other], partner)
    sk_there = link.push(sk.at[own], sk.at[other], partner)

    in_r1.wait()
    e1 = mm_t(go[own, :], r[1, :, 0:width]) + mm_t(sk[own, :], r[1, :, width:])
    es0 = mm_t(sk[own, :], r[0, :, width:])

    halo.wait_recv()
    p0[low, :] = jnp.where(t == 0, jnp.zeros((near, width), BF), p0[low, :])
    layer0(0, near)
    far_low = link.push(xh.at[low], ph.at[low], along(far))
    p0_there = link.push(p0.at[own], p0.at[other], partner)
    x1_there = link.push(xh.at[own, pl.ds(0, width)], xh.at[other, pl.ds(0, width)], partner)
    in_w1.wait()
    zc1 = mm(xh[own, 0:width], w[1, width : 2 * width, :])

    far_high.wait_recv()
    far_low.wait_recv()
    ph[own, :] = jnp.where(t < far, jnp.zeros((rows, width + gated), BF), ph[own, :])
    z1 = zc1 + mm(ph[own, 0:width], w[1, 0:width, :])
    tf = jnp.tanh(z1[:, :gated])
    sg = jax.nn.sigmoid(z1[:, gated:])
    h1 = (tf * sg).astype(BF)
    dza = (e1 * sg * (1.0 - tf * tf)).astype(BF)
    dzb = (e1 * tf * sg * (1.0 - sg)).astype(BF)
    dpast = (mm_t(dza, w[1, 0:width, 0:gated]) + mm_t(dzb, w[1, 0:width, gated:])).astype(BF)
    dp[own, :] = dpast
    back = link.push(dp.at[own], dpr, along(-far))
    first = c == 0
    dz1[own, :] = jnp.where(first, dza, dzb)
    dz1s[...] = jnp.where(first, dzb, dza)
    dz1_there = link.push(dz1s, dz1.at[other], partner)
    half = gated // 2
    for i, hv in enumerate((h1, xh[own, width:], ph[own, width:])):
        lo, hi = hv[:, :half], hv[:, half:]
        hk[i, own, :] = jnp.where(first, lo, hi)
        hs[i] = jnp.where(first, hi, lo)
    hk_there = link.push(hs, hk.at[:, other, :], partner)
    dp_there = link.push(dp.at[own], dp.at[other], partner)
    p1_there = link.push(ph.at[own, pl.ds(0, width)], ph.at[other, pl.ds(0, width)], partner)
    gpv = go[own, :].astype(F32) + (
        mm_t(dza, w[1, width : 2 * width, 0:gated]) + mm_t(dzb, w[1, width : 2 * width, gated:])
    )
    gp[...] = gpv
    gpb[own, :] = gpv.astype(BF)
    gpb_there = link.push(gpb.at[own], gpb.at[other], partner)

    go_there.wait_recv()
    sk_there.wait_recv()
    hk_there.wait_recv()
    dp_there.wait_recv()
    res1a = t_mm(hk[0], go[...])
    res1b = t_mm(hk[0], sk[...])
    res0b = t_mm(hk[1], sk[...])
    gpb_there.wait_recv()
    res0a = t_mm(hk[1], gpb[...]) + t_mm(hk[2], dp[...])
    cut = 384
    for i, (a, b) in enumerate(((res0a, res0b), (res1a, res1b))):
        rs[2 * i] = a[:, :cut].astype(BF)
        rs[2 * i + 1, :, 0 : width - cut] = a[:, cut:].astype(BF)
        rs[2 * i + 1, :, width - cut :] = b.astype(BF)

    def to_x(src, dst):
        return [
            link.push(src.at[lax.rem(x + d, NX)], dst.at[d - 1], xs[d - 1]) for d in range(1, NX)
        ]

    def to_z(src, dst):
        return [
            link.push(src.at[lax.rem(z + d, NZ)], dst.at[d - 1], zs[d - 1]) for d in range(1, NZ)
        ]

    def summed(copies, own_part, slots):
        total = own_part.astype(F32)
        for i, copy in enumerate(copies):
            copy.wait_recv()
            total = total + slots[i].astype(F32)
        return total

    def conv_parts(past, cur, dz, out):
        dzv = dz[...]
        for i in range(NX):
            src = past if i < 2 else cur
            col = (i % 2) * 256
            out[i] = t_mm(src[:, col : col + 256], dzv).astype(BF)

    res_x = to_x(rs, rxr)
    dz1_there.wait_recv()
    x1_there.wait_recv()
    p1_there.wait_recv()
    conv_parts(ph, xh, dz1, cs1)
    conv1_x = to_x(cs1, cx1)

    back.wait_recv()
    g1 = gp[...] + jnp.where(t < nt - far, dpr[...].astype(F32), 0.0)
    e0 = mm_t(g1.astype(BF), r[0, :, 0:width]) + es0
    tf = tf0[...]
    sg = sg0[...]
    dza = (e0 * sg * (1.0 - tf * tf)).astype(BF)
    dzb = (e0 * tf * sg * (1.0 - sg)).astype(BF)
    dz0[own, :] = jnp.where(first, dza, dzb)
    dz0s[...] = jnp.where(first, dzb, dza)
    dz0_there = link.push(dz0s, dz0.at[other], partner)
    dpast = (mm_t(dza, w[0, 0:width, 0:gated]) + mm_t(dzb, w[0, 0:width, gated:])).astype(BF)
    dp0[...] = dpast
    halo_back = link.push(dp0.at[low], dp0r, along(-1))

    rzv = summed(res_x, rs[x], rxr).astype(BF)
    for k in range(NZ):
        rz[k] = rzv[16 * k : 16 * k + 16, :]
    res_z = to_z(rz, rzr)

    x0_there.wait_recv()
    p0_there.wait_recv()
    dz0_there.wait_recv()
    conv_parts(p0, x0, dz0, cs0)
    conv0_x = to_x(cs0, cx0)

    wc = mm_t(dza, w[0, width : 2 * width, 0:gated]) + mm_t(dzb, w[0, width : 2 * width, gated:])
    halo_back.wait_recv()
    tail = jnp.where(t < nt - 1, dp0r[...].astype(F32), 0.0)
    moved = jnp.concatenate([dp0[near:, :].astype(F32), tail], axis=0)
    igv[...] = (g1 + wc + moved).astype(BF)
    link.move(igv, ig_out.at[0], last=True)

    def conv_to_z(copies, parts, slots, out, out_slots):
        v = summed(copies, parts[x], slots).astype(BF)
        for k in range(NZ):
            out[k] = v[32 * k : 32 * k + 32, :]
        return to_z(out, out_slots)

    def conv_to_y(copies, parts, slots, out, out_slots):
        v = summed(copies, parts[z], slots).astype(BF)
        out[0] = v[:16, :]
        out[1] = v[16:, :]
        sends = []
        for i, (dy, dc) in enumerate(yc):
            sends.append(
                link.push(out.at[lax.rem(c + dc, NC)], out_slots.at[i], at(dy=dy, dc=dc))
            )
        return sends

    def conv_final(layer, copies, part, slots):
        mine = part[c].astype(F32)
        theirs = jnp.zeros((16, 256), F32)
        for i, (dy, dc) in enumerate(yc):
            copies[i].wait_recv()
            v = slots[i].astype(F32)
            if dc:
                theirs = theirs + v
            else:
                mine = mine + v
        cgv[layer, :, 0:256] = (jnp.where(first, mine, theirs) * factor).astype(BF)
        cgv[layer, :, 256:512] = (jnp.where(first, theirs, mine) * factor).astype(BF)

    conv1_z = conv_to_z(conv1_x, cs1, cx1, cz1, czr1)

    ryv = summed(res_z, rz[z], rzr).astype(BF)
    ry[...] = ryv
    res_y = [link.push(ry, ryr.at[d - 1], ys[d - 1]) for d in range(1, ny)]

    conv0_z = conv_to_z(conv0_x, cs0, cx0, cz0, czr0)
    conv1_y = conv_to_y(conv1_z, cz1, czr1, cy1, cyr1)

    rf = (summed(res_y, ryv, ryr) * factor).astype(BF)
    rg[z] = rf
    res_gz = [link.push(rg.at[z], rg.at[z], device) for device in zs]

    conv0_y = conv_to_y(conv0_z, cz0, czr0, cy0, cyr0)
    for copy in res_gz:
        copy.wait_recv()
    for k in range(NZ):
        rx[x, 16 * k : 16 * k + 16, :] = rg[k]
    res_gx = [link.push(rx.at[x], rx.at[x], device) for device in xs]

    conv_final(1, conv1_y, cy1, cyr1)
    conv_final(0, conv0_y, cy0, cyr0)
    link.move(cgv, cg_out, last=True)

    for copy in res_gx:
        copy.wait_recv()
    res_gc = link.push(rx, rc, partner)
    for i in range(NX):
        place = rg_out.at[i // 2, pl.ds(c * half, half), pl.ds((i % 2) * cut, cut)]
        link.move(rx.at[i], place, last=True)
    res_gc.wait_recv()
    for i in range(NX):
        place = rg_out.at[i // 2, pl.ds((1 - c) * half, half), pl.ds((i % 2) * cut, cut)]
        link.move(rc.at[i], place, last=True)
    link.finish()


def body(signal, conv_weight, res_weight, grad_out, skip_cotangent):
    ny = lax.axis_size("dp")
    total = signal.shape[0] * signal.shape[1] * ny * lax.axis_size(TM)
    factor = float(total) ** (-0.5)
    yc = ny * NC - 1

    def v(shape, dtype=BF):
        return pltpu.VMEM(shape, dtype)

    scratch = [
        v((256, 512)), v((256, 512)), v((2, 1024, 512)), v((2, 256, 768)),
        v((256, 512)), v((256, 256)), v((256, 768)), v((256, 768)),
        v((128, 256), F32), v((128, 256), F32),
        v((3, 256, 128)), v((3, 128, 128)),
        v((256, 256)), v((128, 256)), v((256, 256)), v((128, 256)),
        v((128, 512), F32), v((256, 512)), v((256, 512)), v((128, 512)), v((128, 512)),
        v((32, 512)), v((128, 512)),
    ]
    for _ in range(2):
        scratch += [
            v((4, 256, 256)), v((3, 256, 256)), v((8, 32, 256)), v((7, 32, 256)),
            v((2, 16, 256)), v((yc, 16, 256)),
        ]
    scratch += [v((2, 16, 512))]
    scratch += [
        v((4, 128, 384)), v((3, 128, 384)), v((8, 16, 384)), v((7, 16, 384)),
        v((16, 384)), v((ny - 1, 16, 384)), v((8, 16, 384)), v((4, 128, 384)), v((4, 128, 384)),
    ]
    remote = 96
    scratch += [
        pltpu.SemaphoreType.DMA((remote,)),
        pltpu.SemaphoreType.DMA((remote,)),
        pltpu.SemaphoreType.DMA((24,)),
    ]
    anyspace = pl.BlockSpec(memory_space=pl.ANY)
    return pl.pallas_call(
        functools.partial(kernel, ny, factor),
        out_shape=(
            jax.ShapeDtypeStruct((1, 128, 512), BF),
            jax.ShapeDtypeStruct((2, 16, 512), BF),
            jax.ShapeDtypeStruct((2, 256, 768), BF),
        ),
        in_specs=[anyspace] * 5,
        out_specs=(anyspace,) * 3,
        scratch_shapes=scratch,
        compiler_params=pltpu.CompilerParams(collective_id=0, has_side_effects=True),
        name="step",
    )(signal, conv_weight, res_weight, grad_out, skip_cotangent)


def solution(mesh):
    split = Mesh(mesh.devices.reshape(mesh.shape["dp"], NX, NZ, NC), ("dp", *TM))
    return jax.shard_map(
        body,
        mesh=split,
        in_specs=(P("dp", TM, None), P(), P(), P("dp", TM, None), P("dp", TM, None)),
        out_specs=(P("dp", TM, None), P(None, TM, None), P()),
        check_vma=False,
    )
```

time: 277 us -> 76.4 us (0.28)
  waiting for transfers between devices: 151 us -> 0 us
  starting transfers between devices: 76.7 us -> 0 us
  Pallas kernels: 0 us -> 70.5 us
  blocking collectives: 15.7 us -> 0 us
  matrix products: 11.2 us -> 0 us
  other arithmetic: 8.18 us -> 0 us
  local copies, waits for them, and re-layouts: 11.4 us -> 5 us
    all_to_all x8 -> x0, waiting for transfers between devices: 116 us -> none  [the longest x3 50.2 us: sum_by_axis(): return jnp.sum(lax.all_to_all(own, far, 0, 0, tiled=True), axis=0)]
    pallas_call x0 -> x1, Pallas kernels: none -> 70.5 us  [body(): pl.pallas_call(functools.partial(kernel, ny, factor), out_shape=(jax.Shap...]
    all_to_all x8 -> x0, starting transfers between devices: 59.3 us -> none  [the longest x3 24.8 us: sum_by_axis(): return jnp.sum(lax.all_to_all(own, far, 0, 0, tiled=True), axis=0)]
    ppermute x4 -> x0, waiting for transfers between devices: 35.5 us -> none  [passed_along(): return lax.ppermute(block, axis, route)]
    ppermute x4 -> x0, starting transfers between devices: 17.4 us -> none  [passed_along(): return lax.ppermute(block, axis, route)]
    all_to_all x2 -> x0, blocking collectives: 15.7 us -> none  [sent_and_summed(): parts = lax.all_to_all(split_up(array, dim, peers), axis, 0, 0, tiled=True)]
    dot_general x11 -> x0, matrix products: 11.2 us -> none  [the longest x2 2.79 us: body(): lax.dot_general(outer, res_weight[layer], (((1,), (1,)), ((), ())), prefe...]
    reduce_sum x8 -> x0, other arithmetic: 4.32 us -> none  [the longest x3 4.11 us: sent_and_summed(): return jnp.sum(parts, axis=0)]
  transfers between devices with their start and end apart: 12 -> 0, of which waited for: 11 -> 0; matrix products, arithmetic and copies ran while one was open for 6% -> 0% of each run, Pallas kernels for 0% -> 0%
where the time goes in v1:
time: 76.4 us; the launch traced here: 76.2 us
  Pallas kernels  70.5 us (92%)
  local copies, waits for them, and re-layouts  5 us (7%)
    pallas_call x1, Pallas kernels, body(): pl.pallas_call(functools.partial(kernel, ny, factor), out_shape=(jax.Shap...  70.5 us
    unnamed x3, local copies, waits for them, and re-layouts  5 us

profile of v1, /device:TPU:1, one launch (start us, length us, event | category | flops | bytes accessed | tf_op | source)
XLA Modules:
  0.0 76.2 jit_solution(18315680161325782268)
XLA Ops:
  0.6 70.5 %step.1 = (bf16[1,128,512]{2,1,0:T(8,128)(2,1)}, bf16[2,16,512]{2,1,0:T(8,128)(2,1)}, bf16[2,256,768]{2,1,0:T(8,128)(2,1)}) custom-call(bf16[1,128,512]{2,1,0:T(8,128)(2,1)} %sig.1, bf16[2,1024,512]{2,1,0:T(8,128)(2,1)} %cw.1, bf16[2,256,768]{2,1,0:T(8,128)(2,1)} %rw.1, bf16[1,128,512]{2,1,0:T(8,128)(2,1)} %go_in.1, bf16[1,128,256]{2,1,0:T(8,128)(2,1)} %sk_in.1), custom_call_target="tpu_custom_call" | custom-call | tf_op jit(solution)/shard_map/step/pallas_call | solution.py:374
  71.2 1.6 %copy.11 = bf16[1,128,512]{2,1,0:T(8,128)(2,1)} copy(bf16[1,128,512]{2,1,0:T(8,128)(2,1)} %get-tuple-element.6) | data formatting | bytes 262144
  72.7 1.4 %copy.12 = bf16[2,16,512]{2,1,0:T(8,128)(2,1)} copy(bf16[2,16,512]{2,1,0:T(8,128)(2,1)} %get-tuple-element.7) | data formatting | bytes 65536
  74.1 2.1 %copy.13 = bf16[2,256,768]{2,1,0:T(8,128)(2,1)} copy(bf16[2,256,768]{2,1,0:T(8,128)(2,1)} %get-tuple-element.8) | data formatting | bytes 1572864

commit v2 on v1

v2 whole, which is shorter than its diff:
```python
import functools

import jax
import jax.numpy as jnp
from jax import lax
from jax.experimental import pallas as pl
from jax.experimental.pallas import tpu as pltpu
from jax.sharding import Mesh
from jax.sharding import PartitionSpec as P

TM = ("tm_0", "tm_1", "tm_2")
NX, NZ, NC = 4, 8, 2
MESH = pl.DeviceIdType.MESH
BF = jnp.bfloat16
F32 = jnp.float32


def mm(a, b):
    return jnp.dot(a, b, preferred_element_type=F32)


def mm_t(a, b):
    return lax.dot_general(a, b, (((1,), (1,)), ((), ())), preferred_element_type=F32)


def t_mm(a, b):
    return lax.dot_general(a, b, (((0,), (0,)), ((), ())), preferred_element_type=F32)


def do_if(cond, action):
    if cond is None:
        action()
    else:
        pl.when(cond)(action)


class Group:
    def __init__(self, link, ref, send_if=None, recv_if=None):
        self.send, self.recv = link.send.at[link.n_remote], link.recv.at[link.n_remote]
        link.n_remote += 1
        link.groups.append(self)
        self.ref, self.device = ref, link.device
        self.send_if, self.recv_if = send_if, recv_if

    def copy(self, src, dst, device):
        return pltpu.make_async_remote_copy(
            src_ref=src,
            dst_ref=dst,
            send_sem=self.send,
            recv_sem=self.recv,
            device_id=device,
            device_id_type=MESH,
        )

    def push(self, src, dst, device):
        do_if(self.send_if, lambda: self.copy(src, dst, device).start())
        return self

    def wait(self):
        do_if(self.recv_if, lambda: self.copy(self.ref, self.ref, self.device).wait_recv())

    def wait_sent(self):
        do_if(self.send_if, lambda: self.copy(self.ref, self.ref, self.device).wait_send())


class Links:
    def __init__(self, send, recv, local, device):
        self.send, self.recv, self.local, self.device = send, recv, local, device
        self.n_remote = self.n_local = 0
        self.groups = []
        self.stored = []

    def push(self, src, dst, device, send_if=None, recv_if=None, ref=None):
        return Group(self, dst if ref is None else ref, send_if, recv_if).push(src, dst, device)

    def move(self, src, dst, last=False):
        i = self.n_local
        self.n_local += 1
        copy = pltpu.make_async_copy(src, dst, self.local.at[i])
        copy.start()
        if last:
            self.stored.append(copy)
        return copy

    def finish(self):
        for group in self.groups:
            group.wait_sent()
        for copy in self.stored:
            copy.wait()


def kernel(
    ny, factor,
    sig, cw, rw, go_in, sk_in,
    ig_out, cg_out, rg_out,
    x0, p0, w, r, go, sk, x1, p1, h0, tf0, sg0, hk, hs, dz1, dz1s, dz0, dz0s,
    gp, o0, dp, dpr, dp0, dp0r, igv,
    cs1, cy1, cx1, cxr1, cz1, czr1, cg1,
    cs0, cx0, cz0, czr0, cy0, cyr0, cgv,
    sa, sb, rgo,
    send, recv, local,
):
    y = lax.axis_index("dp")
    x = lax.axis_index("tm_0")
    z = lax.axis_index("tm_1")
    c = lax.axis_index("tm_2")
    t = x * (NZ * NC) + z * NC + c
    nt = NX * NZ * NC
    near = 32
    far = 8
    rows, width = 128, 512
    gated = 256
    half = gated // 2

    def at(dy=0, dx=0, dz=0, dc=0):
        return (
            lax.rem(y + dy, ny), lax.rem(x + dx, NX), lax.rem(z + dz, NZ), lax.rem(c + dc, NC)
        )

    def along(d):
        s = lax.rem(t + (d + nt), nt)
        return (y, s // (NZ * NC), lax.rem(s // NC, NZ), lax.rem(s, NC))

    partner = at(dc=1)
    xs = [at(dx=d) for d in range(1, NX)]
    zs = [at(dz=d) for d in range(1, NZ)]
    ys = [at(dy=d) for d in range(1, ny)]
    yo = [at(dy=d, dc=1) for d in range(ny)]

    link = Links(send, recv, local, partner)
    own, other = pl.ds(0, rows), pl.ds(rows, rows)
    high = pl.ds(near, rows - near)
    low = pl.ds(0, near)
    in_x = link.move(sig.at[0], x0.at[own])
    in_p = link.move(sig.at[0, pl.ds(0, rows - near)], p0.at[high])
    in_w0 = link.move(cw.at[0], w.at[0])
    in_r0 = link.move(rw.at[0], r.at[0])

    barrier = pltpu.get_barrier_semaphore()
    has = {d: (t + d >= 0) & (t + d < nt) for d in (far, -far, 1, -1)}
    greeted = zs + ys + yo + xs

    def greet(device):
        pl.semaphore_signal(barrier, inc=1, device_id=device, device_id_type=MESH)

    for d in (far, -far):
        do_if(has[d], functools.partial(greet, along(d)))
    for device in greeted:
        greet(device)
    count = len(greeted)
    for d in (1, -1):
        do_if(has[d], functools.partial(greet, along(d)))
    for d in (far, -far, 1, -1):
        count = count + has[d].astype(jnp.int32)

    in_go = link.move(go_in.at[0], go.at[own])
    in_sk = link.move(sk_in.at[0], sk.at[own])
    in_r1 = link.move(rw.at[1], r.at[1])
    in_w1 = link.move(cw.at[1], w.at[1])

    def layer0(lo, n):
        part = pl.ds(lo, n)
        zv = mm(p0[part, :], w[0, 0:width, :]) + mm(x0[part, :], w[0, width : 2 * width, :])
        tf = jnp.tanh(zv[:, :gated])
        sg = jax.nn.sigmoid(zv[:, gated:])
        h = (tf * sg).astype(BF)
        tf0[part, :] = tf
        sg0[part, :] = sg
        h0[part, :] = h
        x1[part, :] = (x0[part, :].astype(F32) + mm(h, r[0, :, 0:width])).astype(BF)

    def cleared(ref):
        def clear():
            ref[...] = jnp.zeros(ref.shape, ref.dtype)

        return clear

    do_if(t == 0, cleared(p0.at[low]))
    do_if(t == nt - 1, cleared(dp0r))
    do_if(t >= nt - far, cleared(dpr))
    do_if(t < far, cleared(p1.at[own]))

    in_x.wait()
    in_p.wait()
    in_w0.wait()
    in_r0.wait()
    layer0(near, rows - near)
    in_go.wait()
    in_sk.wait()

    pl.semaphore_wait(barrier, count)
    halo = link.push(x0.at[pl.ds(rows - near, near)], p0.at[low], along(1), has[1], has[-1])
    far_high = link.push(x1.at[high], p1.at[high], along(far), has[far], has[-far])

    in_r1.wait()
    in_w1.wait()
    e1 = mm_t(go[own, :], r[1, :, 0:width]) + mm_t(sk[own, :], r[1, :, width:])
    es0 = mm_t(sk[own, :], r[0, :, width:])

    halo.wait()
    layer0(0, near)
    far_low = link.push(x1.at[low], p1.at[low], along(far), has[far], has[-far])
    first = c == 0
    hk[0, own, :] = jnp.where(first, h0[:, :half], h0[:, half:])
    hs[0] = jnp.where(first, h0[:, half:], h0[:, :half])
    zc1 = mm(x1[own, :], w[1, width : 2 * width, :])

    far_high.wait()
    far_low.wait()
    go_there = link.push(go.at[own], go.at[other], partner)
    sk_there = link.push(sk.at[own], sk.at[other], partner)
    h0_there = link.push(hs.at[0], hk.at[0, other, :], partner)
    x1_there = link.push(x1.at[own], x1.at[other], partner)
    p1_there = link.push(p1.at[own], p1.at[other], partner)
    x0_there = link.push(x0.at[own], x0.at[other], partner)
    p0_there = link.push(p0.at[own], p0.at[other], partner)
    z1 = zc1 + mm(p1[own, :], w[1, 0:width, :])
    tf = jnp.tanh(z1[:, :gated])
    sg = jax.nn.sigmoid(z1[:, gated:])
    h1 = (tf * sg).astype(BF)
    dza = (e1 * sg * (1.0 - tf * tf)).astype(BF)
    dzb = (e1 * tf * sg * (1.0 - sg)).astype(BF)
    dpast = mm_t(dza, w[1, 0:width, 0:gated]) + mm_t(dzb, w[1, 0:width, gated:])
    dp[...] = dpast.astype(BF)
    back = link.push(dp, dpr, along(-far), has[-far], has[far])
    hk[1, own, :] = jnp.where(first, h1[:, :half], h1[:, half:])
    hs[1] = jnp.where(first, h1[:, half:], h1[:, :half])
    h1_there = link.push(hs.at[1], hk.at[1, other, :], partner)
    dz1[own, :] = jnp.where(first, dza, dzb)
    dz1s[...] = jnp.where(first, dzb, dza)
    dz1_there = link.push(dz1s, dz1.at[other], partner)
    wc = mm_t(dza, w[1, width : 2 * width, 0:gated])
    g = go[own, :].astype(F32) + (wc + mm_t(dzb, w[1, width : 2 * width, gated:]))
    gp[...] = g

    def to_x(src, dst):
        group = Group(link, dst)
        for d in range(1, NX):
            group.push(src.at[lax.rem(x + d, NX)], dst.at[d - 1], xs[d - 1])
        return group

    def to_z(src, dst):
        group = Group(link, dst)
        for d in range(1, NZ):
            group.push(src.at[lax.rem(z + d, NZ)], dst.at[d - 1], zs[d - 1])
        return group

    def to_all(src, dst, devices):
        group = Group(link, dst)
        for i, device in enumerate(devices):
            group.push(src, dst.at[i], device)
        return group

    def to_same(ref, i, devices):
        group = Group(link, ref.at[pl.ds(0, len(devices))])
        for device in devices:
            group.push(ref.at[i], ref.at[i], device)
        return group

    def summed(group, own_part, slots):
        group.wait()
        total = own_part.astype(F32)
        for i in range(slots.shape[0]):
            total = total + slots[i].astype(F32)
        return total

    def res_parts(v, buffers):
        parts, slots = buffers[:2]
        cols = v.shape[1] // 2
        for i in range(NX):
            top, left = 64 * (i // 2), cols * (i % 2)
            piece = v[top : top + 64, left : left + cols]
            parts[i] = piece.reshape(8, 8, cols).astype(BF)
        return to_x(parts, slots)

    def res_to_z(copies, buffers):
        parts, slots, out, out_slots = buffers[:4]
        out[...] = summed(copies, parts[x], slots).astype(BF)
        return to_z(out, out_slots)

    def res_to_y(copies, buffers):
        parts, slots, out, out_slots = buffers[2:6]
        out[...] = summed(copies, parts[z], slots).astype(BF)
        return to_all(out, out_slots, ys)

    def res_to_all_z(copies, buffers):
        part, slots, out = buffers[4:7]
        out[z] = (summed(copies, part[...], slots) * factor).astype(BF)
        return to_same(out, z, zs)

    def res_to_all_x(group, buffers):
        part, out, there = buffers[6:9]
        group.wait()
        out[x] = part[...]
        sends = to_same(out, x, xs)
        return sends, link.push(out.at[x], there.at[x], partner, ref=there)

    def res_to_core(state, buffers):
        out, there = buffers[7:9]
        group, sends = state
        group.wait()
        for d in range(1, NX):
            other_x = lax.rem(x + d, NX)
            sends.push(out.at[other_x], there.at[other_x], partner)
        return sends

    def res_pieces(copies, buffers):
        copies.wait()
        for src, core in ((buffers[7], c), (buffers[8], 1 - c)):
            for i in range(NX):
                v = src[i].astype(F32)
                v = v.reshape(64, v.shape[-1]).astype(BF)
                yield pl.ds(pl.multiple_of(core * half + 64 * (i // 2), 64), 64), i % 2, v

    go_there.wait()
    sk_there.wait()
    h0_there.wait()
    h1_there.wait()
    both = [t_mm(hk[1], go[...]), t_mm(hk[1], sk[...]), t_mm(hk[0], sk[...])]
    resa_x = res_parts(jnp.concatenate(both, axis=1), sa)

    def conv_parts(past, cur, dz, out):
        dzv = dz[...]
        for i in range(NX):
            src = past if i < 2 else cur
            col = (i % 2) * 256
            v = t_mm(src[:, col : col + 256], dzv).astype(BF)
            for k in range(NZ):
                for core in range(NC):
                    at_row = 32 * k + 16 * core
                    out[lax.rem(core + c + 1, NC), i, k] = v[at_row : at_row + 16, :]

    def conv_to_x(src, dst):
        return [to_x(src.at[j], dst.at[j]) for j in range(NC)]

    def conv_to_z(j, copies, parts, slots, out, out_slots):
        out[j] = summed(copies[j], parts[j, x], slots.at[j]).astype(BF)
        return to_z(out.at[j], out_slots.at[j])

    def conv_to_y(j, copies, parts, slots, out, out_slots):
        out[j] = summed(copies, parts[j, z], slots.at[j]).astype(BF)
        devices = ys if j else yo
        return to_all(out.at[j], out_slots.at[j, pl.ds(0, len(devices))], devices)

    def conv_final(layer, copies, part, slots):
        mine = summed(copies[1], part[1], slots.at[1, pl.ds(0, ny - 1)])
        theirs = summed(copies[0], jnp.zeros((16, 256), F32), slots.at[0])
        cgv[layer, :, 0:256] = (jnp.where(first, mine, theirs) * factor).astype(BF)
        cgv[layer, :, 256:512] = (jnp.where(first, theirs, mine) * factor).astype(BF)

    dz1_there.wait()
    x1_there.wait()
    p1_there.wait()
    dzv = dz1[...]
    for i in range(NX):
        src = p1 if i < 2 else x1
        col = (i % 2) * 256
        v = t_mm(src[:, col : col + 256], dzv).reshape(NZ, 4, 8, 256)
        for k in range(8):
            cs1[k, i] = v[:, k // 2, :, 128 * (k % 2) : 128 * (k % 2) + 128].astype(BF)
    conv1_y = Group(link, cy1)
    for d in range(1, ny):
        conv1_y.push(cs1.at[lax.rem(y + d, ny)], cy1.at[d - 1], ys[d - 1])
    back.wait()
    g1 = gp[...] + dpr[...].astype(F32)
    o0[own, :] = g1.astype(BF)
    o0_there = link.push(o0.at[own], o0.at[other], partner)
    e0 = mm_t(o0[own, :], r[0, :, 0:width]) + es0
    tf = tf0[...]
    sg = sg0[...]
    dza = (e0 * sg * (1.0 - tf * tf)).astype(BF)
    dzb = (e0 * tf * sg * (1.0 - sg)).astype(BF)
    dz0[own, :] = jnp.where(first, dza, dzb)
    dz0s[...] = jnp.where(first, dzb, dza)
    dz0_there = link.push(dz0s, dz0.at[other], partner)
    dpast = (mm_t(dza, w[0, 0:width, 0:gated]) + mm_t(dzb, w[0, 0:width, gated:])).astype(BF)
    dp0[...] = dpast
    halo_back = link.push(dp0.at[low], dp0r, along(-1), has[-1], has[1])
    resa_z = res_to_z(resa_x, sa)
    o0_there.wait()
    resb_x = res_parts(t_mm(hk[0], o0[...]), sb)
    x0_there.wait()
    p0_there.wait()
    dz0_there.wait()
    conv_parts(p0, x0, dz0, cs0)
    conv0_x = conv_to_x(cs0, cx0)
    wc = mm_t(dza, w[0, width : 2 * width, 0:gated]) + mm_t(dzb, w[0, width : 2 * width, gated:])
    halo_back.wait()
    moved = jnp.concatenate([dp0[near:, :], dp0r[...]], axis=0).astype(F32)
    igv[...] = (g1 + wc + moved).astype(BF)
    link.move(igv, ig_out.at[0], last=True)
    resb_z = res_to_z(resb_x, sb)
    resa_y = res_to_y(resa_z, sa)
    cx1[...] = summed(conv1_y, cs1[y], cy1).astype(BF)
    conv1_x = to_x(cx1, cxr1)
    conv0_z = [conv_to_z(j, conv0_x, cs0, cx0, cz0, czr0) for j in range(NC)]
    cz1[...] = summed(conv1_x, cx1[x], cxr1).astype(BF)
    conv1_z = to_z(cz1, czr1)
    resb_y = res_to_y(resb_z, sb)
    resa_gz = res_to_all_z(resa_y, sa)
    conv0_y = [conv_to_y(j, conv0_z[j], cz0, czr0, cy0, cyr0) for j in range(NC)]
    resb_gz = res_to_all_z(resb_y, sb)
    cg1[c * ny + y] = (summed(conv1_z, cz1[z], czr1) * factor).astype(BF)
    piece = c * ny + y
    conv1_g = to_same(cg1, piece, ys + yo)
    resa_gx = res_to_all_x(resa_gz, sa)
    resb_gx = res_to_all_x(resb_gz, sb)
    conv_final(0, conv0_y, cy0, cyr0)
    conv1_g.wait()
    for core in range(NC):
        for k in range(4):
            left = 256 * core + 128 * (k % 2)
            top = 8 * (k // 2)
            cgv[1, top : top + 8, left : left + 128] = cg1[ny * core + 4 * c + k]
    link.move(cgv, cg_out, last=True)
    resa_gc = res_to_core(resa_gx, sa)
    for place, side, v in res_pieces(resa_gc, sa):
        if side:
            rgo[1, place, width:] = v[:, :256]
            rgo[0, place, width:] = v[:, 256:]
        else:
            rgo[1, place, 0:width] = v
    link.move(rgo.at[1], rg_out.at[1], last=True)
    resb_gc = res_to_core(resb_gx, sb)
    for place, side, v in res_pieces(resb_gc, sb):
        rgo[0, place, 256 * side : 256 * side + 256] = v
    link.move(rgo.at[0], rg_out.at[0], last=True)
    link.finish()


def store(a, b, c, a_out, b_out, c_out, sems):
    copies = [
        pltpu.make_async_copy(src, dst, sems.at[i])
        for i, (src, dst) in enumerate(((a, a_out), (b, b_out), (c, c_out)))
    ]
    for copy in copies:
        copy.start()
    for copy in copies:
        copy.wait()


def body(signal, conv_weight, res_weight, grad_out, skip_cotangent):
    ny = lax.axis_size("dp")
    total = signal.shape[0] * signal.shape[1] * ny * lax.axis_size(TM)
    factor = float(total) ** (-0.5)

    def v(shape, dtype=BF):
        return pltpu.VMEM(shape, dtype)

    def res_scratch(cols):
        return [
            v((4, 8, 8, cols)), v((3, 8, 8, cols)), v((8, 8, cols)), v((7, 8, cols)),
            v((8, cols)), v((ny - 1, 8, cols)), v((8, 8, cols)), v((4, 8, 8, cols)),
            v((4, 8, 8, cols)),
        ]

    remote = 42
    scratch = [
        v((256, 512)), v((256, 512)), v((2, 1024, 512)), v((2, 256, 768)),
        v((256, 512)), v((256, 256)), v((256, 512)), v((256, 512)), v((128, 256)),
        v((128, 256), F32), v((128, 256), F32),
        v((2, 256, 128)), v((2, 128, 128)),
        v((256, 256)), v((128, 256)), v((256, 256)), v((128, 256)),
        v((128, 512), F32), v((256, 512)), v((128, 512)), v((128, 512)), v((128, 512)),
        v((32, 512)), v((128, 512)),
        v((ny, 4, 8, 8, 128)), v((ny - 1, 4, 8, 8, 128)), v((4, 8, 8, 128)), v((3, 8, 8, 128)),
        v((8, 8, 128)), v((7, 8, 128)), v((2 * ny, 8, 128)),
        v((2, 4, 8, 16, 256)), v((2, 3, 8, 16, 256)), v((2, 8, 16, 256)), v((2, 7, 16, 256)),
        v((2, 16, 256)), v((2, ny, 16, 256)), v((2, 16, 512)),
        res_scratch(512), res_scratch(256), v((2, 256, 768)),
        pltpu.SemaphoreType.DMA((remote,)),
        pltpu.SemaphoreType.DMA((remote,)),
        pltpu.SemaphoreType.DMA((12,)),
    ]
    anyspace = pl.BlockSpec(memory_space=pl.ANY)
    results = pl.pallas_call(
        functools.partial(kernel, ny, factor),
        out_shape=(
            jax.ShapeDtypeStruct((1, 128, 512), BF),
            jax.ShapeDtypeStruct((2, 16, 512), BF),
            jax.ShapeDtypeStruct((2, 256, 768), BF),
        ),
        in_specs=[anyspace] * 5,
        out_specs=(anyspace,) * 3,
        scratch_shapes=scratch,
        compiler_params=pltpu.CompilerParams(collective_id=0, has_side_effects=True),
        name="step",
    )(signal, conv_weight, res_weight, grad_out, skip_cotangent)
    return pl.pallas_call(
        store,
        out_shape=tuple(jax.ShapeDtypeStruct(a.shape, a.dtype) for a in results),
        in_specs=[pl.BlockSpec(memory_space=pltpu.VMEM)] * 3,
        out_specs=(anyspace,) * 3,
        scratch_shapes=[pltpu.SemaphoreType.DMA((3,))],
        name="store",
    )(*results)


def solution(mesh):
    split = Mesh(mesh.devices.reshape(mesh.shape["dp"], NX, NZ, NC), ("dp", *TM))
    return jax.shard_map(
        body,
        mesh=split,
        in_specs=(P("dp", TM, None), P(), P(), P("dp", TM, None), P("dp", TM, None)),
        out_specs=(P("dp", TM, None), P(None, TM, None), P()),
        check_vma=False,
    )
```

time: 76.4 us -> 66.6 us (0.87)
  local copies, waits for them, and re-layouts: 5 us -> 0 us
  Pallas kernels: 70.5 us -> 65.8 us
    pallas_call x1, Pallas kernels: 70.5 us -> 63.6 us  [body(): pl.pallas_call(functools.partial(kernel, ny, factor), out_shape=(jax.Shap...]
    unnamed x3 -> x0, local copies, waits for them, and re-layouts: 5 us -> none
    pallas_call x0 -> x1, Pallas kernels: none -> 2.19 us  [body(): pl.pallas_call(store, out_shape=tuple((jax.ShapeDtypeStruct(a.shape, a.dt...]
where the time goes in v2:
time: 66.6 us; the launch traced here: 66.4 us
  Pallas kernels  65.8 us (99%)
    pallas_call x1, Pallas kernels, body(): pl.pallas_call(functools.partial(kernel, ny, factor), out_shape=(jax.Shap...  63.6 us
    pallas_call x1, Pallas kernels, body(): pl.pallas_call(store, out_shape=tuple((jax.ShapeDtypeStruct(a.shape, a.dt...  2.19 us

profile of v2, /device:TPU:1, one launch (start us, length us, event | category | flops | bytes accessed | tf_op | source)
XLA Modules:
  0.0 66.4 jit_solution(15346958180502808925)
XLA Ops:
  0.6 63.6 %step.1 = (bf16[1,128,512]{2,1,0:T(8,128)(2,1)}, bf16[2,16,512]{2,1,0:T(8,128)(2,1)}, bf16[2,256,768]{2,1,0:T(8,128)(2,1)}) custom-call(bf16[1,128,512]{2,1,0:T(8,128)(2,1)} %sig.1, bf16[2,1024,512]{2,1,0:T(8,128)(2,1)} %cw.1, bf16[2,256,768]{2,1,0:T(8,128)(2,1)} %rw.1, bf16[1,128,512]{2,1,0:T(8,128)(2,1)} %go_in.1, bf16[1,128,256]{2,1,0:T(8,128)(2,1)} %sk_in.1), custom_call_target="tpu_custom_call" | custom-call | tf_op jit(solution)/shard_map/step/pallas_call | solution.py:476
  64.2 2.2 %store.1 = (bf16[1,128,512]{2,1,0:T(8,128)(2,1)}, bf16[2,16,512]{2,1,0:T(8,128)(2,1)}, bf16[2,256,768]{2,1,0:T(8,128)(2,1)}) custom-call(bf16[1,128,512]{2,1,0:T(8,128)(2,1)} %get-tuple-element.6.a, bf16[2,16,512]{2,1,0:T(8,128)(2,1)} %get-tuple-element.7.b, bf16[2,256,768]{2,1,0:T(8,128)(2,1)} %get-tuple-element.8.c), custom_call_target="tpu_custom_call" | custom-call | tf_op jit(solution)/shard_map/store/pallas_call | solution.py:489

commit v3 on v2

--- a/solution.py
+++ b/solution.py
@@ -96,7 +96,7 @@
     x0, p0, w, r, go, sk, x1, p1, h0, tf0, sg0, hk, hs, dz1, dz1s, dz0, dz0s,
     gp, o0, dp, dpr, dp0, dp0r, igv,
     cs1, cy1, cx1, cxr1, cz1, czr1, cg1,
-    cs0, cx0, cz0, czr0, cy0, cyr0, cgv,
+    mine0, left0, right0, cy0, cyr0, cgv,
     sa, sb, rgo,
     send, recv, local,
 ):
@@ -278,6 +278,17 @@
         out[...] = summed(copies, parts[x], slots).astype(BF)
         return to_z(out, out_slots)
 
+    def res_direct(v, parts, slots):
+        for i in range(NX):
+            top, left = 64 * (i // 2), 256 * (i % 2)
+            parts[i] = v[top : top + 64, left : left + 256].reshape(8, 8, 256).astype(BF)
+        group = Group(link, slots)
+        for i in range(1, NX * NZ):
+            dx, dz = i // NZ, i % NZ
+            src = parts.at[lax.rem(x + dx, NX), lax.rem(z + dz, NZ)]
+            group.push(src, slots.at[i - 1], at(dx=dx, dz=dz))
+        return group
+
     def res_to_y(copies, buffers):
         parts, slots, out, out_slots = buffers[2:6]
         out[...] = summed(copies, parts[z], slots).astype(BF)
@@ -319,28 +330,26 @@
     both = [t_mm(hk[1], go[...]), t_mm(hk[1], sk[...]), t_mm(hk[0], sk[...])]
     resa_x = res_parts(jnp.concatenate(both, axis=1), sa)
 
-    def conv_parts(past, cur, dz, out):
+    def conv_parts(past, cur, dz):
         dzv = dz[...]
         for i in range(NX):
             src = past if i < 2 else cur
             col = (i % 2) * 256
-            v = t_mm(src[:, col : col + 256], dzv).astype(BF)
-            for k in range(NZ):
-                for core in range(NC):
-                    at_row = 32 * k + 16 * core
-                    out[lax.rem(core + c + 1, NC), i, k] = v[at_row : at_row + 16, :]
-
-    def conv_to_x(src, dst):
-        return [to_x(src.at[j], dst.at[j]) for j in range(NC)]
-
-    def conv_to_z(j, copies, parts, slots, out, out_slots):
-        out[j] = summed(copies[j], parts[j, x], slots.at[j]).astype(BF)
-        return to_z(out.at[j], out_slots.at[j])
-
-    def conv_to_y(j, copies, parts, slots, out, out_slots):
-        out[j] = summed(copies, parts[j, z], slots.at[j]).astype(BF)
-        devices = ys if j else yo
-        return to_all(out.at[j], out_slots.at[j, pl.ds(0, len(devices))], devices)
+            v = t_mm(src[:, col : col + 256], dzv).reshape(NZ, 2, 16, 256)
+            mine0[0][i] = jnp.where(first, v[:, 0], v[:, 1]).astype(BF)
+            rest = jnp.where(first, v[:, 1], v[:, 0]).astype(BF)
+            left0[0][i] = rest[:, :, :128]
+            right0[0][:, i] = rest[:, :, 128:]
+
+    def x_to_z(group, buffers):
+        parts, slots, out, out_slots = buffers
+        out[...] = summed(group, parts[x], slots).astype(BF)
+        return to_z(out, out_slots)
+
+    def z_to_x(group, buffers):
+        parts, slots, out, out_slots = buffers
+        out[...] = summed(group, parts[z], slots).astype(BF)
+        return to_x(out, out_slots)
 
     def conv_final(layer, copies, part, slots):
         mine = summed(copies[1], part[1], slots.at[1, pl.ds(0, ny - 1)])
@@ -361,6 +370,7 @@
     conv1_y = Group(link, cy1)
     for d in range(1, ny):
         conv1_y.push(cs1.at[lax.rem(y + d, ny)], cy1.at[d - 1], ys[d - 1])
+    resa_z = res_to_z(resa_x, sa)
     back.wait()
     g1 = gp[...] + dpr[...].astype(F32)
     o0[own, :] = g1.astype(BF)
@@ -376,36 +386,43 @@
     dpast = (mm_t(dza, w[0, 0:width, 0:gated]) + mm_t(dzb, w[0, 0:width, gated:])).astype(BF)
     dp0[...] = dpast
     halo_back = link.push(dp0.at[low], dp0r, along(-1), has[-1], has[1])
-    resa_z = res_to_z(resa_x, sa)
     o0_there.wait()
-    resb_x = res_parts(t_mm(hk[0], o0[...]), sb)
+    resb_x = res_direct(t_mm(hk[0], o0[...]), sb[0], sb[1])
     x0_there.wait()
     p0_there.wait()
     dz0_there.wait()
-    conv_parts(p0, x0, dz0, cs0)
-    conv0_x = conv_to_x(cs0, cx0)
+    conv_parts(p0, x0, dz0)
+    right_z = to_z(right0[0], right0[1])
+    mine_x = to_x(mine0[0], mine0[1])
+    left_x = to_x(left0[0], left0[1])
     wc = mm_t(dza, w[0, width : 2 * width, 0:gated]) + mm_t(dzb, w[0, width : 2 * width, gated:])
     halo_back.wait()
     moved = jnp.concatenate([dp0[near:, :], dp0r[...]], axis=0).astype(F32)
     igv[...] = (g1 + wc + moved).astype(BF)
     link.move(igv, ig_out.at[0], last=True)
-    resb_z = res_to_z(resb_x, sb)
     resa_y = res_to_y(resa_z, sa)
     cx1[...] = summed(conv1_y, cs1[y], cy1).astype(BF)
     conv1_x = to_x(cx1, cxr1)
-    conv0_z = [conv_to_z(j, conv0_x, cs0, cx0, cz0, czr0) for j in range(NC)]
+    mine_z = x_to_z(mine_x, mine0)
+    left_z = x_to_z(left_x, left0)
+    right_x = z_to_x(right_z, right0)
+    sb[4][...] = summed(resb_x, sb[0][x, z], sb[1]).astype(BF)
+    resb_y = to_all(sb[4], sb[5], ys)
     cz1[...] = summed(conv1_x, cx1[x], cxr1).astype(BF)
     conv1_z = to_z(cz1, czr1)
-    resb_y = res_to_y(resb_z, sb)
     resa_gz = res_to_all_z(resa_y, sa)
-    conv0_y = [conv_to_y(j, conv0_z[j], cz0, czr0, cy0, cyr0) for j in range(NC)]
+    cy0[1] = summed(mine_z, mine0[2][z], mine0[3]).astype(BF)
+    mine_y = to_all(cy0.at[1], cyr0.at[1, pl.ds(0, ny - 1)], ys)
     resb_gz = res_to_all_z(resb_y, sb)
+    cy0[0, :, 0:128] = summed(left_z, left0[2][z], left0[3]).astype(BF)
+    cy0[0, :, 128:256] = summed(right_x, right0[2][x], right0[3]).astype(BF)
+    rest_y = to_all(cy0.at[0], cyr0.at[0], yo)
     cg1[c * ny + y] = (summed(conv1_z, cz1[z], czr1) * factor).astype(BF)
     piece = c * ny + y
     conv1_g = to_same(cg1, piece, ys + yo)
     resa_gx = res_to_all_x(resa_gz, sa)
     resb_gx = res_to_all_x(resb_gz, sb)
-    conv_final(0, conv0_y, cy0, cyr0)
+    conv_final(0, (rest_y, mine_y), cy0, cyr0)
     conv1_g.wait()
     for core in range(NC):
         for k in range(4):
@@ -428,15 +445,26 @@
     link.finish()
 
 
-def store(a, b, c, a_out, b_out, c_out, sems):
-    copies = [
-        pltpu.make_async_copy(src, dst, sems.at[i])
-        for i, (src, dst) in enumerate(((a, a_out), (b, b_out), (c, c_out)))
+def store(*refs):
+    n = (len(refs) - 2) // 3
+    srcs, dsts, kept = refs[:n], refs[n : 2 * n], refs[2 * n : 3 * n]
+    came, went = refs[-2:]
+    parts = [(a, i) for a in range(n) for i in range(srcs[a].shape[0])]
+    loads = [
+        pltpu.make_async_copy(srcs[a].at[i], kept[a].at[i], came.at[k])
+        for k, (a, i) in enumerate(parts)
     ]
-    for copy in copies:
-        copy.start()
-    for copy in copies:
-        copy.wait()
+    stores = [
+        pltpu.make_async_copy(kept[a].at[i], dsts[a].at[i], went.at[k])
+        for k, (a, i) in enumerate(parts)
+    ]
+    for load in loads:
+        load.start()
+    for load, out in zip(loads, stores):
+        load.wait()
+        out.start()
+    for out in stores:
+        out.wait()
 
 
 def body(signal, conv_weight, res_weight, grad_out, skip_cotangent):
@@ -447,9 +475,9 @@
     def v(shape, dtype=BF):
         return pltpu.VMEM(shape, dtype)
 
-    def res_scratch(cols):
+    def res_scratch(cols, first):
         return [
-            v((4, 8, 8, cols)), v((3, 8, 8, cols)), v((8, 8, cols)), v((7, 8, cols)),
+            v((4, 8, 8, cols)), v((*first, 8, cols)), v((8, 8, cols)), v((7, 8, cols)),
             v((8, cols)), v((ny - 1, 8, cols)), v((8, 8, cols)), v((4, 8, 8, cols)),
             v((4, 8, 8, cols)),
         ]
@@ -465,9 +493,11 @@
         v((32, 512)), v((128, 512)),
         v((ny, 4, 8, 8, 128)), v((ny - 1, 4, 8, 8, 128)), v((4, 8, 8, 128)), v((3, 8, 8, 128)),
         v((8, 8, 128)), v((7, 8, 128)), v((2 * ny, 8, 128)),
-        v((2, 4, 8, 16, 256)), v((2, 3, 8, 16, 256)), v((2, 8, 16, 256)), v((2, 7, 16, 256)),
+        [v((4, 8, 16, 256)), v((3, 8, 16, 256)), v((8, 16, 256)), v((7, 16, 256))],
+        [v((4, 8, 16, 128)), v((3, 8, 16, 128)), v((8, 16, 128)), v((7, 16, 128))],
+        [v((8, 4, 16, 128)), v((7, 4, 16, 128)), v((4, 16, 128)), v((3, 16, 128))],
         v((2, 16, 256)), v((2, ny, 16, 256)), v((2, 16, 512)),
-        res_scratch(512), res_scratch(256), v((2, 256, 768)),
+        res_scratch(512, (3, 8)), res_scratch(256, (31,)), v((2, 256, 768)),
         pltpu.SemaphoreType.DMA((remote,)),
         pltpu.SemaphoreType.DMA((remote,)),
         pltpu.SemaphoreType.DMA((12,)),
@@ -486,12 +516,13 @@
         compiler_params=pltpu.CompilerParams(collective_id=0, has_side_effects=True),
         name="step",
     )(signal, conv_weight, res_weight, grad_out, skip_cotangent)
+    n = sum(a.shape[0] for a in results)
     return pl.pallas_call(
         store,
         out_shape=tuple(jax.ShapeDtypeStruct(a.shape, a.dtype) for a in results),
-        in_specs=[pl.BlockSpec(memory_space=pltpu.VMEM)] * 3,
+        in_specs=[anyspace] * 3,
         out_specs=(anyspace,) * 3,
-        scratch_shapes=[pltpu.SemaphoreType.DMA((3,))],
+        scratch_shapes=[v(a.shape) for a in results] + [pltpu.SemaphoreType.DMA((n,))] * 2,
         name="store",
     )(*results)
 

time: 66.6 us -> 64.2 us (0.964)
  Pallas kernels: 65.8 us -> 63.4 us
    pallas_call x1, Pallas kernels: 63.6 us -> 61.4 us  [body(): pl.pallas_call(functools.partial(kernel, ny, factor), out_shape=(jax.Shap...]
where the time goes in v3:
time: 64.2 us; the launch traced here: 64.1 us
  Pallas kernels  63.4 us (99%)
    pallas_call x1, Pallas kernels, body(): pl.pallas_call(functools.partial(kernel, ny, factor), out_shape=(jax.Shap...  61.4 us
    pallas_call x1, Pallas kernels, body(): pl.pallas_call(store, out_shape=tuple((jax.ShapeDtypeStruct(a.shape, a.dt...  2.07 us

profile of v3, /device:TPU:1, one launch (start us, length us, event | category | flops | bytes accessed | tf_op | source)
XLA Modules:
  0.0 64.1 jit_solution(18051881364231316638)
XLA Ops:
  0.6 61.4 %step.1 = (bf16[1,128,512]{2,1,0:T(8,128)(2,1)}, bf16[2,16,512]{2,1,0:T(8,128)(2,1)}, bf16[2,256,768]{2,1,0:T(8,128)(2,1)}) custom-call(bf16[1,128,512]{2,1,0:T(8,128)(2,1)} %sig.1, bf16[2,1024,512]{2,1,0:T(8,128)(2,1)} %cw.1, bf16[2,256,768]{2,1,0:T(8,128)(2,1)} %rw.1, bf16[1,128,512]{2,1,0:T(8,128)(2,1)} %go_in.1, bf16[1,128,256]{2,1,0:T(8,128)(2,1)} %sk_in.1), custom_call_target="tpu_custom_call" | custom-call | tf_op jit(solution)/shard_map/step/pallas_call | solution.py:506
  62.0 2.1 %store.1 = (bf16[1,128,512]{2,1,0:T(8,128)(2,1)}, bf16[2,16,512]{2,1,0:T(8,128)(2,1)}, bf16[2,256,768]{2,1,0:T(8,128)(2,1)}) custom-call(bf16[1,128,512]{2,1,0:T(8,128)(2,1)} %get-tuple-element.6.refs_0_, bf16[2,16,512]{2,1,0:T(8,128)(2,1)} %get-tuple-element.7.refs_1_, bf16[2,256,768]{2,1,0:T(8,128)(2,1)} %get-tuple-element.8.refs_2_), custom_call_target="tpu_custom_call" | custom-call | tf_op jit(solution)/shard_map/store/pallas_call | solution.py:520

commit v4 on v3

--- a/solution.py
+++ b/solution.py
@@ -1,4 +1,5 @@
 import functools
+import math
 
 import jax
 import jax.numpy as jnp
@@ -36,9 +37,14 @@
 
 class Group:
     def __init__(self, link, ref, send_if=None, recv_if=None):
-        self.send, self.recv = link.send.at[link.n_remote], link.recv.at[link.n_remote]
+        self.recv = link.recv.at[link.n_remote]
         link.n_remote += 1
-        link.groups.append(self)
+        if send_if is None:
+            self.send = link.send.at[0]
+            link.total += math.prod(ref.shape)
+        else:
+            link.groups.append(self)
+            self.send = link.send.at[len(link.groups)]
         self.ref, self.device = ref, link.device
         self.send_if, self.recv_if = send_if, recv_if
 
@@ -64,9 +70,10 @@
 
 
 class Links:
-    def __init__(self, send, recv, local, device):
+    def __init__(self, send, recv, local, device, spare):
         self.send, self.recv, self.local, self.device = send, recv, local, device
-        self.n_remote = self.n_local = 0
+        self.spare = spare
+        self.n_remote = self.n_local = self.total = 0
         self.groups = []
         self.stored = []
 
@@ -85,6 +92,15 @@
     def finish(self):
         for group in self.groups:
             group.wait_sent()
+        assert self.total % 256 == 0
+        pltpu.make_async_remote_copy(
+            src_ref=self.spare.at[pl.ds(0, self.total // 256)],
+            dst_ref=self.spare.at[pl.ds(0, self.total // 256)],
+            send_sem=self.send.at[0],
+            recv_sem=self.recv.at[0],
+            device_id=self.device,
+            device_id_type=MESH,
+        ).wait_send()
         for copy in self.stored:
             copy.wait()
 
@@ -97,7 +113,7 @@
     gp, o0, dp, dpr, dp0, dp0r, igv,
     cs1, cy1, cx1, cxr1, cz1, czr1, cg1,
     mine0, left0, right0, cy0, cyr0, cgv,
-    sa, sb, rgo,
+    sa, sb, rgo, spare,
     send, recv, local,
 ):
     y = lax.axis_index("dp")
@@ -127,7 +143,7 @@
     ys = [at(dy=d) for d in range(1, ny)]
     yo = [at(dy=d, dc=1) for d in range(ny)]
 
-    link = Links(send, recv, local, partner)
+    link = Links(send, recv, local, partner, spare)
     own, other = pl.ds(0, rows), pl.ds(rows, rows)
     high = pl.ds(near, rows - near)
     low = pl.ds(0, near)
@@ -207,13 +223,14 @@
 
     far_high.wait()
     far_low.wait()
-    go_there = link.push(go.at[own], go.at[other], partner)
-    sk_there = link.push(sk.at[own], sk.at[other], partner)
-    h0_there = link.push(hs.at[0], hk.at[0, other, :], partner)
-    x1_there = link.push(x1.at[own], x1.at[other], partner)
-    p1_there = link.push(p1.at[own], p1.at[other], partner)
-    x0_there = link.push(x0.at[own], x0.at[other], partner)
-    p0_there = link.push(p0.at[own], p0.at[other], partner)
+    inputs = (hk.at[0, other, :], go.at[other], sk.at[other])
+    rest = (x1.at[other], p1.at[other], x0.at[other], p0.at[other])
+    words = sum(math.prod(ref.shape) for ref in inputs + rest)
+    shared = Group(link, spare.at[pl.ds(0, words // 256)])
+    for src, dst in zip((hs.at[0], go.at[own], sk.at[own]), inputs):
+        shared.push(src, dst, partner)
+    for ref, dst in zip((x1, p1, x0, p0), rest):
+        shared.push(ref.at[own], dst, partner)
     z1 = zc1 + mm(p1[own, :], w[1, 0:width, :])
     tf = jnp.tanh(z1[:, :gated])
     sg = jax.nn.sigmoid(z1[:, gated:])
@@ -323,9 +340,7 @@
                 v = v.reshape(64, v.shape[-1]).astype(BF)
                 yield pl.ds(pl.multiple_of(core * half + 64 * (i // 2), 64), 64), i % 2, v
 
-    go_there.wait()
-    sk_there.wait()
-    h0_there.wait()
+    shared.wait()
     h1_there.wait()
     both = [t_mm(hk[1], go[...]), t_mm(hk[1], sk[...]), t_mm(hk[0], sk[...])]
     resa_x = res_parts(jnp.concatenate(both, axis=1), sa)
@@ -358,8 +373,6 @@
         cgv[layer, :, 256:512] = (jnp.where(first, theirs, mine) * factor).astype(BF)
 
     dz1_there.wait()
-    x1_there.wait()
-    p1_there.wait()
     dzv = dz1[...]
     for i in range(NX):
         src = p1 if i < 2 else x1
@@ -383,27 +396,25 @@
     dz0[own, :] = jnp.where(first, dza, dzb)
     dz0s[...] = jnp.where(first, dzb, dza)
     dz0_there = link.push(dz0s, dz0.at[other], partner)
-    dpast = (mm_t(dza, w[0, 0:width, 0:gated]) + mm_t(dzb, w[0, 0:width, gated:])).astype(BF)
-    dp0[...] = dpast
-    halo_back = link.push(dp0.at[low], dp0r, along(-1), has[-1], has[1])
     o0_there.wait()
     resb_x = res_direct(t_mm(hk[0], o0[...]), sb[0], sb[1])
-    x0_there.wait()
-    p0_there.wait()
     dz0_there.wait()
     conv_parts(p0, x0, dz0)
     right_z = to_z(right0[0], right0[1])
     mine_x = to_x(mine0[0], mine0[1])
     left_x = to_x(left0[0], left0[1])
+    dpast = (mm_t(dza, w[0, 0:width, 0:gated]) + mm_t(dzb, w[0, 0:width, gated:])).astype(BF)
+    dp0[...] = dpast
+    halo_back = link.push(dp0.at[low], dp0r, along(-1), has[-1], has[1])
     wc = mm_t(dza, w[0, width : 2 * width, 0:gated]) + mm_t(dzb, w[0, width : 2 * width, gated:])
+    resa_y = res_to_y(resa_z, sa)
+    cx1[...] = summed(conv1_y, cs1[y], cy1).astype(BF)
+    conv1_x = to_x(cx1, cxr1)
+    mine_z = x_to_z(mine_x, mine0)
     halo_back.wait()
     moved = jnp.concatenate([dp0[near:, :], dp0r[...]], axis=0).astype(F32)
     igv[...] = (g1 + wc + moved).astype(BF)
     link.move(igv, ig_out.at[0], last=True)
-    resa_y = res_to_y(resa_z, sa)
-    cx1[...] = summed(conv1_y, cs1[y], cy1).astype(BF)
-    conv1_x = to_x(cx1, cxr1)
-    mine_z = x_to_z(mine_x, mine0)
     left_z = x_to_z(left_x, left0)
     right_x = z_to_x(right_z, right0)
     sb[4][...] = summed(resb_x, sb[0][x, z], sb[1]).astype(BF)
@@ -482,7 +493,7 @@
             v((4, 8, 8, cols)),
         ]
 
-    remote = 42
+    remote = 33
     scratch = [
         v((256, 512)), v((256, 512)), v((2, 1024, 512)), v((2, 256, 768)),
         v((256, 512)), v((256, 256)), v((256, 512)), v((256, 512)), v((128, 256)),
@@ -497,8 +508,8 @@
         [v((4, 8, 16, 128)), v((3, 8, 16, 128)), v((8, 16, 128)), v((7, 16, 128))],
         [v((8, 4, 16, 128)), v((7, 4, 16, 128)), v((4, 16, 128)), v((3, 16, 128))],
         v((2, 16, 256)), v((2, ny, 16, 256)), v((2, 16, 512)),
-        res_scratch(512, (3, 8)), res_scratch(256, (31,)), v((2, 256, 768)),
-        pltpu.SemaphoreType.DMA((remote,)),
+        res_scratch(512, (3, 8)), res_scratch(256, (31,)), v((2, 256, 768)), v((8192, 256)),
+        pltpu.SemaphoreType.DMA((6,)),
         pltpu.SemaphoreType.DMA((remote,)),
         pltpu.SemaphoreType.DMA((12,)),
     ]

time: 64.2 us -> 63.5 us (0.989)
  Pallas kernels: 63.4 us -> 62.7 us
    pallas_call x1, Pallas kernels: 61.4 us -> 60.6 us  [body(): pl.pallas_call(functools.partial(kernel, ny, factor), out_shape=(jax.Shap...]
where the time goes in v4:
time: 63.5 us; the launch traced here: 63.4 us
  Pallas kernels  62.7 us (99%)
  between operations  0.64 us (1%)
    pallas_call x1, Pallas kernels, body(): pl.pallas_call(functools.partial(kernel, ny, factor), out_shape=(jax.Shap...  60.6 us
    pallas_call x1, Pallas kernels, body(): pl.pallas_call(store, out_shape=tuple((jax.ShapeDtypeStruct(a.shape, a.dt...  2.07 us

profile of v4, /device:TPU:1, one launch (start us, length us, event | category | flops | bytes accessed | tf_op | source)
XLA Modules:
  0.0 63.4 jit_solution(16744533219158726439)
XLA Ops:
  0.6 60.6 %step.1 = (bf16[1,128,512]{2,1,0:T(8,128)(2,1)}, bf16[2,16,512]{2,1,0:T(8,128)(2,1)}, bf16[2,256,768]{2,1,0:T(8,128)(2,1)}) custom-call(bf16[1,128,512]{2,1,0:T(8,128)(2,1)} %sig.1, bf16[2,1024,512]{2,1,0:T(8,128)(2,1)} %cw.1, bf16[2,256,768]{2,1,0:T(8,128)(2,1)} %rw.1, bf16[1,128,512]{2,1,0:T(8,128)(2,1)} %go_in.1, bf16[1,128,256]{2,1,0:T(8,128)(2,1)} %sk_in.1), custom_call_target="tpu_custom_call" | custom-call | tf_op jit(solution)/shard_map/step/pallas_call | solution.py:517
  61.3 2.1 %store.1 = (bf16[1,128,512]{2,1,0:T(8,128)(2,1)}, bf16[2,16,512]{2,1,0:T(8,128)(2,1)}, bf16[2,256,768]{2,1,0:T(8,128)(2,1)}) custom-call(bf16[1,128,512]{2,1,0:T(8,128)(2,1)} %get-tuple-element.6.refs_0_, bf16[2,16,512]{2,1,0:T(8,128)(2,1)} %get-tuple-element.7.refs_1_, bf16[2,256,768]{2,1,0:T(8,128)(2,1)} %get-tuple-element.8.refs_2_), custom_call_target="tpu_custom_call" | custom-call | tf_op jit(solution)/shard_map/store/pallas_call | solution.py:531
